TPU v7x, 32 devices: a whole 2x2x4 slice. The times are simulated.
32 devices in a mesh: role: 4 (over y, core), shard: 8 (over z, x).
Axes of the slice: x: 2, y: 2, z: 4, core: 2. Of those that a mesh axis runs over, the one named last changes fastest.
Arguments:
- gradient: bfloat16 [2560, 2560], P('shard', 'role'), may hold values from -1200 to 1200
- left_old: float32 [2560, 2560], P('shard', 'role'), may hold values from -1 to 10, as said below
- right_old: float32 [2560, 2560], P('shard', 'role'), may hold values from -1 to 10, as said below
- basis_old: bfloat16 [2560, 512], P('shard', 'role'), may hold values from -1 to 1
Outputs:
- left_stat: float32 [2560, 2560], P('shard', 'role')
- right_stat: float32 [2560, 2560], P('shard', 'role')
- left_basis: float32 [2560, 512], P('shard', 'role')
Inputs may be any that keep to these rules, and one draw needn't show every extreme that they name: `left_old`: symmetric and positive definite. `right_old`: symmetric and positive definite.
All inputs are finite; a program needn't handle non-finite values.
Results may differ from a plain program's by a relative error of at most 0.0003.
Values may be sent and summed in bfloat16 or wider, within the bound.
No kernel may reach another device: no remote copies, remote signals or barrier semaphores. Data moves between devices by JAX's collectives and lax.ppermute only.
A program may use at most 64 MiB of HBM per device.

v0:
```python
import jax
import jax.numpy as jnp
from jax import lax
from jax.sharding import PartitionSpec as P

smoothing = 0.95
clip_ratio = 4.0
epsilon_value = 1e-06


def lower_gram(power_row, role_count, role_at):
    order_size = power_row.shape[1]
    tile_size = order_size // (2 * role_count)
    second_row = 2 * role_count - 1 - role_at

    def strip(tile_row):
        chosen = lax.dynamic_slice_in_dim(power_row, tile_row * tile_size, tile_size, 1)
        return lax.dot_general(
            chosen,
            power_row,
            (((0,), (0,)), ((), ())),
            precision=lax.Precision.HIGHEST,
            preferred_element_type=jnp.float32,
        )

    strip_first = strip(role_at)
    strip_second = strip(second_row)
    split_at = (role_at + 1) * tile_size
    packed_width = order_size + tile_size
    first_ext = jnp.concatenate(
        [strip_first, jnp.zeros((tile_size, tile_size), jnp.float32)], axis=1
    )
    padded_second = jnp.concatenate(
        [jnp.zeros((tile_size, order_size), jnp.float32), strip_second], axis=1
    )
    second_ext = lax.dynamic_slice_in_dim(padded_second, order_size - split_at, packed_width, 1)
    columns = lax.broadcasted_iota(jnp.int32, (tile_size, packed_width), 1)
    packed = jnp.where(columns < split_at, first_ext, second_ext)
    tile_sums = lax.psum(packed, "shard")
    strips = lax.all_gather(tile_sums, "role", axis=0, tiled=True)
    lower_part = jnp.zeros((order_size, order_size), jnp.float32)
    for member in range(role_count):
        packed_row = strips[member * tile_size : (member + 1) * tile_size]
        head = (member + 1) * tile_size
        other = 2 * role_count - 1 - member
        tail = (2 * role_count - member) * tile_size
        lower_part = lower_part.at[member * tile_size : head, :head].set(packed_row[:, :head])
        lower_part = lower_part.at[other * tile_size : (other + 1) * tile_size, :tail].set(
            packed_row[:, head : head + tail]
        )
    return jnp.tril(lower_part) + jnp.transpose(jnp.tril(lower_part, -1))


def on_device(gradient, left_old, right_old, basis_old):
    row_count, col_count = gradient.shape
    vec_count = basis_old.shape[1]
    order_size = row_count * lax.axis_size("shard")
    role_count = lax.axis_size("role")
    role_at = lax.axis_index("role")
    col_start = role_at * col_count
    vec_start = role_at * vec_count
    gradient_wide = gradient.astype(jnp.float32)
    squares = lax.psum(jnp.sum(gradient_wide * gradient_wide), ("role", "shard"))
    factor = jnp.minimum(
        1.0, clip_ratio * jnp.sqrt(jnp.float32(order_size)) / jnp.sqrt(squares + epsilon_value)
    )
    squared = factor * factor
    grad_row = lax.all_gather(gradient, "role", axis=1, tiled=True)
    left_part = lax.dot_general(
        gradient,
        lax.all_gather(gradient, "shard", axis=0, tiled=True),
        (((1,), (1,)), ((), ())),
        preferred_element_type=jnp.float32,
    )
    right_share = lax.psum_scatter(
        lax.dot_general(
            grad_row, gradient, (((0,), (0,)), ((), ())), preferred_element_type=jnp.float32
        ),
        "shard",
        scatter_dimension=0,
        tiled=True,
    )
    placed = lax.dynamic_update_slice_in_dim(
        jnp.zeros((row_count, order_size), jnp.float32), left_old, col_start, 1
    )
    left_row = lax.psum((1.0 - smoothing) * squared * left_part + smoothing * placed, "role")
    left_stat = lax.dynamic_slice_in_dim(left_row, col_start, col_count, 1)
    right_stat = smoothing * right_old + (1.0 - smoothing) * squared * right_share
    power_block = jnp.dot(
        left_row,
        lax.all_gather(basis_old, "shard", axis=0, tiled=True).astype(jnp.float32),
        precision=lax.Precision.HIGHEST,
    )
    power_row = lax.all_gather(power_block, "role", axis=1, tiled=True)
    gram_full = lower_gram(power_row, role_count, role_at)
    factor_lower = jnp.linalg.cholesky(gram_full)
    solved = jax.scipy.linalg.solve_triangular(factor_lower, power_row.T, lower=True)
    left_basis = lax.dynamic_slice_in_dim(solved, vec_start, vec_count, 0).T
    return (left_stat, right_stat, left_basis)


def solution(mesh):
    return jax.shard_map(
        on_device,
        mesh=mesh,
        in_specs=(P("shard", "role"), P("shard", "role"), P("shard", "role"), P("shard", "role")),
        out_specs=(P("shard", "role"), P("shard", "role"), P("shard", "role")),
        check_vma=False,
    )
```

profile of v0, /device:TPU:0, one launch (start us, length us, event | category | flops | bytes accessed | tf_op | source)
XLA Modules:
  0.0 411.2 jit_solution(2077507508806869421)
XLA Ops:
  7.2 0.7 all-gather.3.cloned.1.call-update
  7.9 1.8 multiply_reduce_fusion
  9.8 44.0 %psum.21 = f32[]{:T(128)} all-reduce(f32[]{:T(128)} %multiply_reduce_fusion), channel_id=1, replica_groups=mesh['role'=4,'shard'=8] {'role','shard'}, use_global_device_ids=true, to_apply=%region_1.0 | all-reduce | flops 1 | bytes 8 | tf_op jit(solution)/shard_map/psum | solution.py:63
  54.8 0.8 copy-done.2
  55.7 20.1 %all-gather.3.cloned.1.call-done = bf16[2560,640]{1,0:T(8,128)(2,1)} async-done(((bf16[320,640]{1,0:T(8,128)(2,1)}), bf16[2560,640]{1,0:T(8,128)(2,1)}) %all-gather.3.cloned.1.call-update) | async-done | bytes 3276816 | tf_op jit(solution)/shard_map/all_gather | solution.py:71
  75.8 5.2 %fusion = f32[320,2560]{1,0:T(8,128)} fusion(bf16[320,640]{1,0:T(8,128)(2,1)} %param.20, bf16[2560,640]{1,0:T(8,128)(2,1)} %all-gather.3.cloned.1.call-done, f32[320,2560]{1,0:T(8,128)S(1)} %constant_dynamic-update-slice_fusion.1, f32[]{:T(128)S(6)} %mul.51), kind=kOutput, calls=%fused_computation.3 | convolution fusion | flops 1051033600 | bytes 10240004 | tf_op jit(solution)/shard_map/dot_general | solution.py:69
  81.1 0.7 all-gather.5.cloned.1.call-update
  81.9 31.9 %all_gather.17 = bf16[2560,128]{1,0:T(8,128)(2,1)S(1)} all-gather(bf16[320,128]{1,0:T(8,128)(2,1)S(1)} %copy-done.3), channel_id=1, replica_groups=mesh['role'=4,'shard'=8] {'shard'}, dimensions={0}, use_global_device_ids=true | all-gather | bytes 737280 | tf_op jit(solution)/shard_map/all_gather | solution.py:91
  113.8 36.7 %all-reduce.7.cloned.1.call-done = f32[320,2560]{1,0:T(8,128)} async-done(((f32[320,2560]{1,0:T(8,128)}), f32[320,2560]{1,0:T(8,128)}) %all-reduce.7.cloned.1.call-update) | async-done | bytes 3276816 | tf_op jit(solution)/shard_map/psum | solution.py:86
  150.5 3.5 fusion.45
  154.0 7.2 %all_gather.18 = f32[320,512]{1,0:T(8,128)S(1)} all-gather(f32[320,128]{1,0:T(8,128)S(1)} %fusion.45), channel_id=1, replica_groups=mesh['role'=4,'shard'=8] {'role'}, dimensions={1}, use_global_device_ids=true | all-gather | bytes 819200 | tf_op jit(solution)/shard_map/all_gather | solution.py:94
  161.2 0.6 fusion.23
  161.8 0.6 fusion.25
  162.5 0.8 fusion.16
  163.3 8.9 %all-gather.5.cloned.1.call-done = bf16[320,2560]{1,0:T(8,128)(2,1)} async-done(((bf16[320,640]{1,0:T(8,128)(2,1)}), bf16[320,2560]{1,0:T(8,128)(2,1)}) %all-gather.5.cloned.1.call-update) | async-done | bytes 1638416 | tf_op jit(solution)/shard_map/all_gather | solution.py:68
  172.2 6.3 %fusion.44 = f32[2560,640]{1,0:T(8,128)} fusion(bf16[320,2560]{1,0:T(8,128)(2,1)} %all-gather.5.cloned.1.call-done, bf16[320,640]{1,0:T(8,128)(2,1)S(1)} %copy-done), kind=kOutput, calls=%fused_computation.97 | convolution fusion | flops 1048576000 | bytes 8601600 | tf_op jit(solution)/shard_map/dot_general | solution.py:76
  178.5 2.1 constant_dynamic-slice_fusion.1
  180.6 65.4 %all-reduce.9.cloned.1.call-done = f32[64,576]{1,0:T(8,128)} async-done(((f32[64,576]{1,0:T(8,128)}), f32[64,576]{1,0:T(8,128)}) %all-reduce.9.cloned.1.call-update) | async-done | bytes 147472 | tf_op jit(solution)/shard_map/psum | solution.py:39
  246.0 8.1 %all_gather.19 = f32[256,576]{1,0:T(8,128)S(1)} all-gather(f32[64,576]{1,0:T(8,128)} %all-reduce.9.cloned.1.call-done), channel_id=1, replica_groups=mesh['role'=4,'shard'=8] {'role'}, dimensions={0}, use_global_device_ids=true | all-gather | bytes 737280 | tf_op jit(solution)/shard_map/all_gather | solution.py:40
  254.4 1.7 scatter.31
  256.0 1.6 scatter.34
  257.8 2.1 scatter.39
  260.0 1.3 copy.7
  261.4 1.4 bitcast_add_fusion.1
  263.4 1.0 copy-done.1
  264.4 11.7 %cholesky.103 = f32[128,128]{1,0:T(8,128)S(1)} custom-call(f32[128,128]{1,0:T(8,128)S(1)} %cholesky.263), custom_call_target="Cholesky" | custom-call | tf_op jit(solution)/shard_map/jit(cholesky)/cholesky | solution.py:96
  276.2 9.8 %custom-call.31 = f32[1,128,128]{1,2,0:T(8,128)S(1)} custom-call(f32[1,128,128]{2,1,0:T(8,128)S(1)} %get-tuple-element.126), custom_call_target="InvertDiagBlocksLowerTriangular" | custom-call | tf_op jit(solution)/shard_map/jit(cholesky)/cholesky | solution.py:96
  286.1 1.2 constant_dynamic-update-slice_fusion
  287.3 1.3 convolution_subtract_fusion
  288.6 11.7 %cholesky.215 = f32[128,128]{1,0:T(8,128)S(1)} custom-call(f32[128,128]{1,0:T(8,128)S(1)} %cholesky.267), custom_call_target="Cholesky" | custom-call | tf_op jit(solution)/shard_map/jit(cholesky)/cholesky | solution.py:96
  300.4 10.0 %custom-call.32 = f32[1,128,128]{1,2,0:T(8,128)S(1)} custom-call(f32[1,128,128]{2,1,0:T(8,128)S(1)} %get-tuple-element.123), custom_call_target="InvertDiagBlocksLowerTriangular" | custom-call | tf_op jit(solution)/shard_map/jit(cholesky)/cholesky | solution.py:96
  310.6 1.3 convolution_subtract_fusion.4
  311.9 11.7 %cholesky.236 = f32[128,128]{1,0:T(8,128)S(1)} custom-call(f32[128,128]{1,0:T(8,128)S(1)} %cholesky.272), custom_call_target="Cholesky" | custom-call | tf_op jit(solution)/shard_map/jit(cholesky)/cholesky | solution.py:96
  323.6 9.8 %custom-call.33 = f32[1,128,128]{1,2,0:T(8,128)S(1)} custom-call(f32[1,128,128]{2,1,0:T(8,128)S(1)} %get-tuple-element.120), custom_call_target="InvertDiagBlocksLowerTriangular" | custom-call | tf_op jit(solution)/shard_map/jit(cholesky)/cholesky | solution.py:96
  333.7 1.2 convolution_subtract_fusion.5
  334.9 11.9 %cholesky.253 = f32[128,128]{1,0:T(8,128)S(1)} custom-call(f32[128,128]{1,0:T(8,128)S(1)} %convolution_subtract_fusion.5), custom_call_target="Cholesky" | custom-call | tf_op jit(solution)/shard_map/jit(cholesky)/cholesky | solution.py:96
  346.8 0.7 compare_reduce_fusion.2
  348.8 0.6 compare_reduce_fusion.1
  350.1 0.6 compare_reduce_fusion
  351.5 8.0 %while.9 = (s32[]{:T(128)}, f32[512,512]{1,0:T(8,128)S(1)}, s32[4,2]{0,1:T(2,128)S(1)}, f32[4,128,128]{2,1,0:T(8,128)S(1)}, s32[]{:T(128)}) while((s32[]{:T(128)}, f32[512,512]{1,0:T(8,128)S(1)}, s32[4,2]{0,1:T(2,128)S(1)}, f32[4,128,128]{2,1,0:T(8,128)S(1)}, s32[]{:T(128)}) %tuple.63), condition=%wide.while_cond.8, body=%wide.while_body.8.sunk | while | flops 2 | bytes 131181 | solution.py:97
  352.1 1.4 bitcast_dynamic-update-slice_fusion.2
  354.1 1.4 bitcast_dynamic-update-slice_fusion.2
  356.2 1.4 bitcast_dynamic-update-slice_fusion.2
  358.2 1.4 bitcast_dynamic-update-slice_fusion.2
  359.6 39.3 %custom-call.34 = f32[4,128,128]{1,2,0:T(8,128)S(1)} custom-call(f32[4,128,128]{2,1,0:T(8,128)S(1)} %get-tuple-element.106), custom_call_target="InvertDiagBlocksLowerTriangular" | custom-call | tf_op jit(solution)/shard_map/jit(_solve_triangular)/triangular_solve | solution.py:97
  400.5 0.6 convolution_subtract_fusion.1
  401.4 0.7 fusion.20
  402.1 2.4 multiply_add_fusion
  (59 shorter events, 7.0 us)
Async XLA Ops:
  7.2 68.6 %all-gather.3.cloned.1.call-start = ((), (), s32[]{:S(2)}) async-start(), calls=%async_computation.1 | async-start | bytes 3686400 | tf_op jit(solution)/shard_map/all_gather | solution.py:71
  7.9 142.6 %all-reduce.7.cloned.1.call-start = ((), (), s32[]{:S(2)}) async-start(), calls=%async_computation.2 | async-start | bytes 6553600 | tf_op jit(solution)/shard_map/psum | solution.py:86
  54.4 1.1 copy-start.2
  81.0 0.9 copy-start.3
  81.0 91.2 %all-gather.5.cloned.1.call-start = ((), (), s32[]{:S(2)}) async-start(), calls=%async_computation.3 | async-start | bytes 2048000 | tf_op jit(solution)/shard_map/all_gather | solution.py:68
  81.8 164.2 %all-reduce.9.cloned.1.call-start = ((), (), s32[]{:S(2)}) async-start(), calls=%async_computation.5 | async-start | bytes 327680 | tf_op jit(solution)/shard_map/psum | solution.py:39
  113.8 58.4 %copy-start = (bf16[320,640]{1,0:T(8,128)(2,1)S(1)}, bf16[320,640]{1,0:T(8,128)(2,1)}, u32[]{:S(2)}) copy-start(bf16[320,640]{1,0:T(8,128)(2,1)} %param.20) | copy-start | bytes 1228804
  163.3 238.8 %reduce-scatter.2.cloned.1.call-start = ((), (), s32[]{:S(2)}) async-start(), calls=%async_computation.4 | async-start | bytes 7372800 | tf_op jit(solution)/shard_map/reduce_scatter | solution.py:75
  263.4 1.0 copy-start.1
Sparse Core Ops, SparseCore 0:
  10.2 65.5 all-gather.2
  81.1 69.3 all-reduce.6
  152.1 20.0 all-gather.4
  176.0 69.9 all-reduce.8
  249.5 121.9 reduce-scatter.1
where the time goes:
time: 419 us; the launch traced here: 411 us
  waiting for transfers between devices  132 us (32%)
  other arithmetic  126 us (30%)
  blocking collectives  91.2 us (22%)
  matrix products  24.1 us (6%)
  local copies, waits for them, and re-layouts  19.9 us (5%)
  between operations  17.7 us (4%)
    another operation x14, other arithmetic, on_device(): factor_lower = jnp.linalg.cholesky(gram_full)  78.7 us
    psum x1, waiting for transfers between devices, lower_gram(): tile_sums = lax.psum(packed, 'shard')  65.4 us
    psum x1, blocking collectives, on_device(): lax.psum(jnp.sum(gradient_wide * gradient_wide), ('role', 'shard'))  44 us
    another operation x3, other arithmetic, on_device(): jax.scipy.linalg.solve_triangular(factor_lower, power_row.T, lower=True)  39.4 us
    psum x1, waiting for transfers between devices, on_device(): lax.psum((1.0 - smoothing) * squared * left_part + smoothing * placed, 'r...  36.7 us
    all_gather x1, blocking collectives, on_device(): lax.all_gather(basis_old, 'shard', axis=0, tiled=True).astype(jnp.float32)  31.9 us
    all_gather x1, waiting for transfers between devices, on_device(): lax.all_gather(gradient, 'shard', axis=0, tiled=True)  20.1 us
    all_gather x1, waiting for transfers between devices, on_device(): grad_row = lax.all_gather(gradient, 'role', axis=1, tiled=True)  8.91 us
  transfers between devices with their start and end apart: 5, of which 4 were waited for; matrix products, arithmetic and copies ran while one was open for 39% of the time, Pallas kernels for 0%

commit v1 on v0

--- a/solution.py
+++ b/solution.py
@@ -2,6 +2,7 @@
 import jax.numpy as jnp
 from jax import lax
 from jax.sharding import PartitionSpec as P
+from jax.lax import axis_size, ppermute
 
 smoothing = 0.95
 clip_ratio = 4.0
@@ -36,7 +37,23 @@
     second_ext = lax.dynamic_slice_in_dim(padded_second, order_size - split_at, packed_width, 1)
     columns = lax.broadcasted_iota(jnp.int32, (tile_size, packed_width), 1)
     packed = jnp.where(columns < split_at, first_ext, second_ext)
-    tile_sums = lax.psum(packed, "shard")
+
+    def _choose_masks(field_in):
+        wide_n = axis_size("shard")
+
+        def match_types(moved, shaped):
+            if shaped >= wide_n:
+                return moved
+            store = []
+            for i0 in tuple(range(wide_n)):
+                store.append((i0, i0 ^ shaped))
+            y_new = match_types(moved + ppermute(moved, "shard", perm=store), 2 * shaped)
+            return y_new
+
+        arr_out = match_types(field_in, 1)
+        return arr_out
+
+    tile_sums = _choose_masks(packed)
     strips = lax.all_gather(tile_sums, "role", axis=0, tiled=True)
     lower_part = jnp.zeros((order_size, order_size), jnp.float32)
     for member in range(role_count):

time: 419 us -> 402 us (0.959)
  waiting for transfers between devices: 132 us -> 111 us
    psum x1 -> x0, waiting for transfers between devices: 65.4 us -> none  [lower_gram(): tile_sums = lax.psum(packed, 'shard')]
    ppermute x0 -> x3, waiting for transfers between devices: none -> 42.2 us  [match_types(): ppermute(moved, 'shard', perm=store)]
    all_gather x1, waiting for transfers between devices: 8.91 us -> 14.9 us  [on_device(): grad_row = lax.all_gather(gradient, 'role', axis=1, tiled=True)]
  transfers between devices with their start and end apart: 5 -> 7, of which waited for: 4 -> 6; matrix products, arithmetic and copies ran while one was open for 39% -> 42% of each run, Pallas kernels for 0% -> 0%
where the time goes in v1:
time: 402 us; the launch traced here: 394 us
  other arithmetic  125 us (31%)
  waiting for transfers between devices  111 us (28%)
  blocking collectives  91.1 us (23%)
  matrix products  24.2 us (6%)
  local copies, waits for them, and re-layouts  20.7 us (5%)
  between operations  17.7 us (4%)
  starting transfers between devices  4.17 us (1%)
    another operation x14, other arithmetic, on_device(): factor_lower = jnp.linalg.cholesky(gram_full)  78.7 us
    psum x1, blocking collectives, on_device(): lax.psum(jnp.sum(gradient_wide * gradient_wide), ('role', 'shard'))  44.2 us
    ppermute x3, waiting for transfers between devices, match_types(): ppermute(moved, 'shard', perm=store)  42.2 us
    another operation x3, other arithmetic, on_device(): jax.scipy.linalg.solve_triangular(factor_lower, power_row.T, lower=True)  39.4 us
    psum x1, waiting for transfers between devices, on_device(): lax.psum((1.0 - smoothing) * squared * left_part + smoothing * placed, 'r...  33.9 us
    all_gather x1, blocking collectives, on_device(): lax.all_gather(basis_old, 'shard', axis=0, tiled=True).astype(jnp.float32)  32 us
    all_gather x1, waiting for transfers between devices, on_device(): lax.all_gather(gradient, 'shard', axis=0, tiled=True)  19.1 us
    all_gather x1, waiting for transfers between devices, on_device(): grad_row = lax.all_gather(gradient, 'role', axis=1, tiled=True)  14.9 us
  transfers between devices with their start and end apart: 7, of which 6 were waited for; matrix products, arithmetic and copies ran while one was open for 42% of the time, Pallas kernels for 0%

profile of v1, /device:TPU:0, one launch (start us, length us, event | category | flops | bytes accessed | tf_op | source)
XLA Modules:
  0.0 394.3 jit_solution(18165228630254049292)
XLA Ops:
  7.2 0.7 all-gather.3.cloned.1.call-update
  7.9 0.7 all-gather.5.cloned.1.call-update
  8.7 1.8 multiply_reduce_fusion
  10.5 44.2 %psum.14 = f32[]{:T(128)} all-reduce(f32[]{:T(128)} %multiply_reduce_fusion), channel_id=1, replica_groups=mesh['role'=4,'shard'=8] {'role','shard'}, use_global_device_ids=true, to_apply=%region_1.0 | all-reduce | flops 1 | bytes 8 | tf_op jit(solution)/shard_map/psum | solution.py:80
  55.8 0.8 copy-done.2
  56.6 19.1 %all-gather.3.cloned.1.call-done = bf16[2560,640]{1,0:T(8,128)(2,1)} async-done(((bf16[320,640]{1,0:T(8,128)(2,1)}), bf16[2560,640]{1,0:T(8,128)(2,1)}) %all-gather.3.cloned.1.call-update) | async-done | bytes 3276816 | tf_op jit(solution)/shard_map/all_gather | solution.py:88
  75.7 5.3 %fusion = f32[320,2560]{1,0:T(8,128)} fusion(bf16[320,640]{1,0:T(8,128)(2,1)} %param.20, bf16[2560,640]{1,0:T(8,128)(2,1)} %all-gather.3.cloned.1.call-done, f32[320,2560]{1,0:T(8,128)S(1)} %constant_dynamic-update-slice_fusion.1, f32[]{:T(128)S(6)} %mul.51), kind=kOutput, calls=%fused_computation.3 | convolution fusion | flops 1051033600 | bytes 10240004 | tf_op jit(solution)/shard_map/dot_general | solution.py:86
  81.0 14.9 %all-gather.5.cloned.1.call-done = bf16[320,2560]{1,0:T(8,128)(2,1)} async-done(((bf16[320,640]{1,0:T(8,128)(2,1)}), bf16[320,2560]{1,0:T(8,128)(2,1)}) %all-gather.5.cloned.1.call-update) | async-done | bytes 1638416 | tf_op jit(solution)/shard_map/all_gather | solution.py:85
  96.0 6.3 %fusion.44 = f32[2560,640]{1,0:T(8,128)} fusion(bf16[320,2560]{1,0:T(8,128)(2,1)} %all-gather.5.cloned.1.call-done, bf16[320,640]{1,0:T(8,128)(2,1)S(1)} %copy-done), kind=kOutput, calls=%fused_computation.97 | convolution fusion | flops 1048576000 | bytes 8601600 | tf_op jit(solution)/shard_map/dot_general | solution.py:93
  102.3 0.8 copy-done.3
  103.1 32.0 %all_gather.17 = bf16[2560,128]{1,0:T(8,128)(2,1)S(1)} all-gather(bf16[320,128]{1,0:T(8,128)(2,1)S(1)} %copy-done.3), channel_id=1, replica_groups=mesh['role'=4,'shard'=8] {'shard'}, dimensions={0}, use_global_device_ids=true | all-gather | bytes 737280 | tf_op jit(solution)/shard_map/all_gather | solution.py:108
  135.1 33.9 %all-reduce.6.cloned.1.call-done = f32[320,2560]{1,0:T(8,128)} async-done(((f32[320,2560]{1,0:T(8,128)}), f32[320,2560]{1,0:T(8,128)}) %all-reduce.6.cloned.1.call-update) | async-done | bytes 3276816 | tf_op jit(solution)/shard_map/psum | solution.py:103
  169.0 3.5 fusion.45
  172.4 7.2 %all_gather.18 = f32[320,512]{1,0:T(8,128)S(1)} all-gather(f32[320,128]{1,0:T(8,128)S(1)} %fusion.45), channel_id=1, replica_groups=mesh['role'=4,'shard'=8] {'role'}, dimensions={1}, use_global_device_ids=true | all-gather | bytes 819200 | tf_op jit(solution)/shard_map/all_gather | solution.py:111
  181.0 1.5 collective-permute-start
  182.5 8.9 %collective-permute-done = f32[64,576]{1,0:T(8,128)S(1)} collective-permute-done((f32[64,576]{1,0:T(8,128)S(1)}, f32[64,576]{1,0:T(8,128)S(1)}, u32[]{:S(2)}, u32[]{:S(2)}) %collective-permute-start) | collective-permute-done | bytes 147488 | tf_op jit(solution)/shard_map/ppermute | solution.py:50
  191.5 1.6 collective-permute-start.1
  193.1 15.2 %collective-permute-done.1 = f32[64,576]{1,0:T(8,128)S(1)} collective-permute-done((f32[64,576]{1,0:T(8,128)S(1)}, f32[64,576]{1,0:T(8,128)S(1)}, u32[]{:S(2)}, u32[]{:S(2)}) %collective-permute-start.1) | collective-permute-done | bytes 147488 | tf_op jit(solution)/shard_map/ppermute | solution.py:50
  208.3 0.9 collective-permute-start.2
  209.2 2.1 constant_dynamic-slice_fusion.1
  211.4 18.0 %collective-permute-done.2 = f32[64,576]{1,0:T(8,128)S(1)} collective-permute-done((f32[64,576]{1,0:T(8,128)S(1)}, f32[64,576]{1,0:T(8,128)S(1)}, u32[]{:S(2)}, u32[]{:S(2)}) %collective-permute-start.2) | collective-permute-done | bytes 147488 | tf_op jit(solution)/shard_map/ppermute | solution.py:50
  229.5 7.7 %all_gather.19 = f32[256,576]{1,0:T(8,128)S(1)} all-gather(f32[64,576]{1,0:T(8,128)S(1)} %add.129), channel_id=1, replica_groups=mesh['role'=4,'shard'=8] {'role'}, dimensions={0}, use_global_device_ids=true | all-gather | bytes 737280 | tf_op jit(solution)/shard_map/all_gather | solution.py:57
  237.5 1.7 scatter.31
  239.2 1.6 scatter.34
  240.9 2.1 scatter.39
  243.2 1.3 copy.7
  244.5 1.4 bitcast_add_fusion.1
  246.5 1.0 copy-done.1
  247.5 11.7 %cholesky.103 = f32[128,128]{1,0:T(8,128)S(1)} custom-call(f32[128,128]{1,0:T(8,128)S(1)} %cholesky.263), custom_call_target="Cholesky" | custom-call | tf_op jit(solution)/shard_map/jit(cholesky)/cholesky | solution.py:113
  259.4 9.8 %custom-call.31 = f32[1,128,128]{1,2,0:T(8,128)S(1)} custom-call(f32[1,128,128]{2,1,0:T(8,128)S(1)} %get-tuple-element.126), custom_call_target="InvertDiagBlocksLowerTriangular" | custom-call | tf_op jit(solution)/shard_map/jit(cholesky)/cholesky | solution.py:113
  269.2 1.2 constant_dynamic-update-slice_fusion
  270.4 1.3 convolution_subtract_fusion
  271.7 11.7 %cholesky.215 = f32[128,128]{1,0:T(8,128)S(1)} custom-call(f32[128,128]{1,0:T(8,128)S(1)} %cholesky.267), custom_call_target="Cholesky" | custom-call | tf_op jit(solution)/shard_map/jit(cholesky)/cholesky | solution.py:113
  283.5 10.0 %custom-call.32 = f32[1,128,128]{1,2,0:T(8,128)S(1)} custom-call(f32[1,128,128]{2,1,0:T(8,128)S(1)} %get-tuple-element.123), custom_call_target="InvertDiagBlocksLowerTriangular" | custom-call | tf_op jit(solution)/shard_map/jit(cholesky)/cholesky | solution.py:113
  293.7 1.3 convolution_subtract_fusion.4
  295.0 11.7 %cholesky.236 = f32[128,128]{1,0:T(8,128)S(1)} custom-call(f32[128,128]{1,0:T(8,128)S(1)} %cholesky.272), custom_call_target="Cholesky" | custom-call | tf_op jit(solution)/shard_map/jit(cholesky)/cholesky | solution.py:113
  306.8 9.8 %custom-call.33 = f32[1,128,128]{1,2,0:T(8,128)S(1)} custom-call(f32[1,128,128]{2,1,0:T(8,128)S(1)} %get-tuple-element.120), custom_call_target="InvertDiagBlocksLowerTriangular" | custom-call | tf_op jit(solution)/shard_map/jit(cholesky)/cholesky | solution.py:113
  316.8 1.2 convolution_subtract_fusion.5
  318.0 11.9 %cholesky.253 = f32[128,128]{1,0:T(8,128)S(1)} custom-call(f32[128,128]{1,0:T(8,128)S(1)} %convolution_subtract_fusion.5), custom_call_target="Cholesky" | custom-call | tf_op jit(solution)/shard_map/jit(cholesky)/cholesky | solution.py:113
  329.9 0.7 compare_reduce_fusion.2
  334.6 8.0 %while.9 = (s32[]{:T(128)}, f32[512,512]{1,0:T(8,128)S(1)}, s32[4,2]{0,1:T(2,128)S(1)}, f32[4,128,128]{2,1,0:T(8,128)S(1)}, s32[]{:T(128)}) while((s32[]{:T(128)}, f32[512,512]{1,0:T(8,128)S(1)}, s32[4,2]{0,1:T(2,128)S(1)}, f32[4,128,128]{2,1,0:T(8,128)S(1)}, s32[]{:T(128)}) %tuple.63), condition=%wide.while_cond.8, body=%wide.while_body.8.sunk | while | flops 2 | bytes 131181 | solution.py:114
  335.3 1.4 bitcast_dynamic-update-slice_fusion.2
  337.3 1.4 bitcast_dynamic-update-slice_fusion.2
  339.3 1.4 bitcast_dynamic-update-slice_fusion.2
  341.3 1.4 bitcast_dynamic-update-slice_fusion.2
  342.7 39.3 %custom-call.34 = f32[4,128,128]{1,2,0:T(8,128)S(1)} custom-call(f32[4,128,128]{2,1,0:T(8,128)S(1)} %get-tuple-element.106), custom_call_target="InvertDiagBlocksLowerTriangular" | custom-call | tf_op jit(solution)/shard_map/jit(_solve_triangular)/triangular_solve | solution.py:114
  384.5 0.7 fusion.20
  385.2 2.4 multiply_add_fusion
  (65 shorter events, 10.1 us)
Async XLA Ops:
  7.2 68.5 %all-gather.3.cloned.1.call-start = ((), (), s32[]{:S(2)}) async-start(), calls=%async_computation.1 | async-start | bytes 3686400 | tf_op jit(solution)/shard_map/all_gather | solution.py:88
  7.9 88.1 %all-gather.5.cloned.1.call-start = ((), (), s32[]{:S(2)}) async-start(), calls=%async_computation.3 | async-start | bytes 2048000 | tf_op jit(solution)/shard_map/all_gather | solution.py:85
  8.6 160.3 %all-reduce.6.cloned.1.call-start = ((), (), s32[]{:S(2)}) async-start(), calls=%async_computation.2 | async-start | bytes 6553600 | tf_op jit(solution)/shard_map/psum | solution.py:103
  55.4 1.1 copy-start.2
  81.0 15.0 %copy-start = (bf16[320,640]{1,0:T(8,128)(2,1)S(1)}, bf16[320,640]{1,0:T(8,128)(2,1)}, u32[]{:S(2)}) copy-start(bf16[320,640]{1,0:T(8,128)(2,1)} %param.20) | copy-start | bytes 1228804
  81.0 304.2 %reduce-scatter.2.cloned.1.call-start = ((), (), s32[]{:S(2)}) async-start(), calls=%async_computation.4 | async-start | bytes 7372800 | tf_op jit(solution)/shard_map/reduce_scatter | solution.py:92
  102.2 0.9 copy-start.3
  181.0 10.5 %collective-permute-start = (f32[64,576]{1,0:T(8,128)S(1)}, f32[64,576]{1,0:T(8,128)S(1)}, u32[]{:S(2)}, u32[]{:S(2)}) collective-permute-start(f32[64,576]{1,0:T(8,128)S(1)} %fusion.16), channel_id=1, source_target_pairs={{0,1},{1,0},{2,3},{3,2},{4,5},{5,4},{6,7},{7,6},{8,9},{9,8},{10,11... | collective-permute-start | bytes 442376 | tf_op jit(solution)/shard_map/ppermute | solution.py:50
  191.5 16.8 %collective-permute-start.1 = (f32[64,576]{1,0:T(8,128)S(1)}, f32[64,576]{1,0:T(8,128)S(1)}, u32[]{:S(2)}, u32[]{:S(2)}) collective-permute-start(f32[64,576]{1,0:T(8,128)S(1)} %add.127), channel_id=1, source_target_pairs={{0,2},{1,3},{2,0},{3,1},{4,6},{5,7},{6,4},{7,5},{8,10},{9,11},{10,... | collective-permute-start | bytes 442376 | tf_op jit(solution)/shard_map/ppermute | solution.py:50
  208.3 21.1 %collective-permute-start.2 = (f32[64,576]{1,0:T(8,128)S(1)}, f32[64,576]{1,0:T(8,128)S(1)}, u32[]{:S(2)}, u32[]{:S(2)}) collective-permute-start(f32[64,576]{1,0:T(8,128)S(1)} %add.128), channel_id=1, source_target_pairs={{0,4},{1,5},{2,6},{3,7},{4,0},{5,1},{6,2},{7,3},{8,12},{9,13},{10,... | collective-permute-start | bytes 442376 | tf_op jit(solution)/shard_map/ppermute | solution.py:50
  246.5 1.0 copy-start.1
Sparse Core Ops, SparseCore 0:
  10.2 65.4 all-gather.2
  77.2 18.6 all-gather.4
  98.3 70.5 all-reduce.5
  172.4 132.0 reduce-scatter.1
